TPU v7x, 128 devices: a whole 4x4x4 slice. The times are simulated.
128 devices in a mesh: req: 16 (over y, x), seq: 8 (over z, core).
Axes of the slice: x: 4, y: 4, z: 4, core: 2. Of those that a mesh axis runs over, the one named last changes fastest.
Arguments:
- qkv_proj: bfloat16 [16, 1024, 4096], P('req', 'seq'), may hold values from -6 to 6
- gate_proj: bfloat16 [16, 1024, 2048], P('req', 'seq'), may hold values from -6 to 6
- residual: bfloat16 [16, 1024, 2048], P('req', 'seq'), may hold values from -6 to 6
- log_decay: float32 [16, 1024, 8], P('req', 'seq'), may hold values from -1 to 0, as said below
- beta_logit: bfloat16 [16, 1024, 8], P('req', 'seq'), may hold values from -6 to 6
- lengths: int32 [16], replicated, may hold values from 1 to 1024, 8192 in all
- slot_request: int32 [16], replicated, may hold values from 0 to 15, each once
- conv_weight: float32 [4, 4096], replicated, may hold values from -3 to 3
- norm_gain: float32 [256], replicated, may hold values from 0.1 to 1.9
- out_weight: bfloat16 [2048, 2048], P(('req', 'seq')), may hold values from -0.125 to 0.125
- mlp_gain: float32 [2048], replicated, may hold values from 0.1 to 1.9
- w_gate: bfloat16 [2048, 5632], P('req', 'seq'), may hold values from -0.125 to 0.125
- w_up: bfloat16 [2048, 5632], P('req', 'seq'), may hold values from -0.125 to 0.125
- w_down: bfloat16 [5632, 2048], P('seq', 'req'), may hold values from -0.078125 to 0.078125
Outputs:
- hidden_out: bfloat16 [16, 1024, 2048], P('req', 'seq')
- final_state: float32 [16, 8, 128, 256], P('req', 'seq')
- conv_edge: bfloat16 [16, 3, 4096], P('req', None, 'seq')
Inputs may be any that keep to these rules, and one draw needn't show every extreme that they name: Slot s of the req axis holds request slot_request[s]. The 16 lengths sum to 8192, and the longest is exactly 1024. `log_decay`: every entry is negative.
All inputs are finite; a program needn't handle non-finite values.
Results may differ from a plain program's by a relative error of at most 0.014.
Values may be sent and summed in bfloat16 or wider, within the bound.
A program may use at most 128 MiB of HBM per device.

v0:
```python
import jax
import jax.numpy as jnp
from jax import lax
from jax.sharding import PartitionSpec as P

LOCAL_HEADS = 8
DK = 128
DV = 256
CONV = 4
BLOCK = 64
HK = 1024
EPS_NORM = 1e-05
EPS_UNIT = 1e-06
HIGHEST = lax.Precision.HIGHEST


def shifted(value, axis, steps):
    count = lax.axis_size(axis)
    initial, last = (max(0, -steps), min(count, count - steps))
    return lax.ppermute(value, axis, [(source, source + steps) for source in range(initial, last)])


def unit_norm(vector):
    return vector * lax.rsqrt(jnp.sum(vector * vector, axis=-1, keepdims=True) + EPS_UNIT)


def to_blocks(tensor, block_len):
    length = tensor.shape[0]
    grouped = tensor.reshape((length // block_len, block_len) + tensor.shape[1:])
    return jnp.moveaxis(grouped, 2, 0)


def block_tables(query_vec, key_vecs, beta_gate, decay_log, block_len):
    query_b = to_blocks(query_vec, block_len)
    keys_b = to_blocks(key_vecs, block_len)
    beta_b = to_blocks(beta_gate, block_len)
    cumulative = jnp.cumsum(to_blocks(decay_log, block_len), axis=-1)
    spread = cumulative[..., :, None] - cumulative[..., None, :]
    lower_full = jnp.tril(jnp.ones((block_len, block_len), jnp.float32))
    lower_strict = jnp.tril(jnp.ones((block_len, block_len), jnp.float32), -1)
    within = jnp.exp(jnp.where(lower_full > 0, spread, 0.0)) * lower_full
    key_inner = jnp.einsum("hnik,hnjk->hnij", keys_b, keys_b, precision=HIGHEST)
    couple = beta_b[..., :, None] * within * lower_strict * key_inner
    identity = jnp.broadcast_to(jnp.eye(block_len, dtype=jnp.float32), couple.shape)
    inverse = lax.linalg.triangular_solve(
        identity + couple, identity, left_side=True, lower=True, unit_diagonal=True
    )
    growth = jnp.exp(cumulative)
    weighted_keys = jnp.einsum(
        "hnij,hnjk->hnik", inverse, (beta_b * growth)[..., None] * keys_b, precision=HIGHEST
    )
    query_keys = jnp.einsum("hnik,hnjk->hnij", query_b, keys_b, precision=HIGHEST) * within
    grown_query = growth[..., None] * query_b
    keys_to_end = jnp.exp(cumulative[..., -1:] - cumulative)[..., None] * keys_b
    end_growth = growth[..., -1]
    return (inverse, beta_b, (weighted_keys, query_keys, grown_query, keys_to_end, end_growth))


def solve_values(inverse, beta_b, values_b):
    return jnp.einsum("hnij,hnjx->hnix", inverse, beta_b[..., None] * values_b, precision=HIGHEST)


def run_blocks(initial, solved, tables):
    weighted_keys, query_keys, grown_query, keys_to_end, end_growth = tables
    sequence = tuple(
        (
            jnp.moveaxis(tensor, 1, 0)
            for tensor in (solved, weighted_keys, query_keys, grown_query, keys_to_end, end_growth)
        )
    )

    def advance(running, inputs_now):
        solved_now, weighted_now, inner_now, query_now, keys_now, growth_now = inputs_now
        corrected = solved_now - jnp.einsum(
            "hck,hkx->hcx", weighted_now, running, precision=HIGHEST
        )
        output_now = jnp.einsum("hck,hkx->hcx", query_now, running, precision=HIGHEST) + jnp.einsum(
            "hcd,hdx->hcx", inner_now, corrected, precision=HIGHEST
        )
        running = growth_now[:, None, None] * running + jnp.einsum(
            "hck,hcx->hkx", keys_now, corrected, precision=HIGHEST
        )
        return (running, output_now)

    return lax.scan(advance, initial, sequence)


def local(
    qkv_proj,
    gate_proj,
    residual,
    log_decay,
    beta_logit,
    lengths,
    slot_request,
    conv_weight,
    norm_gain,
    out_weight,
    mlp_gain,
    w_gate,
    w_up,
    w_down,
):
    seq_index = lax.axis_index("seq")
    req_index = lax.axis_index("req")
    seq_size = lax.axis_size("seq")
    piece_len = qkv_proj.shape[1]
    channels = qkv_proj.shape[2]
    request_ids = jnp.arange(slot_request.shape[0], dtype=jnp.int32)
    request = jnp.sum(jnp.where(request_ids == req_index, slot_request, 0))
    length = jnp.sum(jnp.where(request_ids == request, lengths, 0))
    position = seq_index * piece_len + jnp.arange(piece_len, dtype=jnp.int32)
    live_mask = position < length
    tokens = qkv_proj[0]
    rim_rows = shifted(tokens[piece_len - (CONV - 1) :], "seq", 1)
    extended = jnp.concatenate([rim_rows, tokens], axis=0)
    convolved = jnp.zeros((piece_len, channels), jnp.float32)
    for offset in range(CONV):
        convolved = convolved + conv_weight[offset] * extended[offset : offset + piece_len].astype(
            jnp.float32
        )
    activated = jax.nn.silu(convolved)
    query_vec = unit_norm(activated[:, :HK].reshape(piece_len, LOCAL_HEADS, DK)) * DK ** (-0.5)
    key_vecs = unit_norm(activated[:, HK : 2 * HK].reshape(piece_len, LOCAL_HEADS, DK))
    values = activated[:, 2 * HK :].reshape(piece_len, LOCAL_HEADS, DV)
    beta_gate = jax.nn.sigmoid(beta_logit[0].astype(jnp.float32)) * live_mask[:, None]
    decay_log = jnp.where(live_mask[:, None], log_decay[0], 0.0)
    inverse, beta_b, tables = block_tables(query_vec, key_vecs, beta_gate, decay_log, BLOCK)
    values_b = to_blocks(values, BLOCK)
    solved = solve_values(inverse, beta_b, values_b)
    zero_state = jnp.zeros((LOCAL_HEADS, DK, DV), jnp.float32)
    incoming = zero_state
    for section_index in range(seq_size - 1):
        ending, discarded = run_blocks(incoming, solved, tables)
        incoming = shifted(ending.astype(jnp.bfloat16), "seq", 1).astype(ending.dtype)
    ending, outputs = run_blocks(incoming, solved, tables)
    outputs = jnp.moveaxis(outputs, 1, 2).reshape(piece_len, LOCAL_HEADS, DV)
    is_last = seq_index == seq_size - 1
    state_term = jnp.where(is_last, ending, 0.0)
    targets = length - (CONV - 1) + jnp.arange(CONV - 1, dtype=jnp.int32)
    select = (position[None, :] == targets[:, None]).astype(jnp.bfloat16)
    edge_term = jnp.dot(select, tokens, preferred_element_type=jnp.float32)
    state_part, edge_part = (
        lax.psum_scatter(
            state_term.astype(jnp.bfloat16), "seq", scatter_dimension=0, tiled=True
        ).astype(jnp.float32),
        lax.psum_scatter(
            edge_term.astype(jnp.bfloat16), "seq", scatter_dimension=1, tiled=True
        ).astype(jnp.float32),
    )
    gate_values = gate_proj[0].astype(jnp.float32).reshape(piece_len, LOCAL_HEADS, DV)
    scaled = outputs * lax.rsqrt(jnp.mean(outputs * outputs, axis=-1, keepdims=True) + EPS_NORM)
    mixed_heads = (
        (scaled * norm_gain * jax.nn.silu(gate_values))
        .reshape(piece_len, LOCAL_HEADS * DV)
        .astype(jnp.bfloat16)
    )
    attended = jnp.dot(
        mixed_heads,
        lax.all_gather(out_weight, ("req", "seq"), axis=0, tiled=True),
        preferred_element_type=jnp.float32,
    )
    hidden_state = (residual[0].astype(jnp.float32) + attended).astype(jnp.bfloat16)
    stream = hidden_state.astype(jnp.float32)
    normed = (
        stream * lax.rsqrt(jnp.mean(stream * stream, axis=-1, keepdims=True) + EPS_NORM) * mlp_gain
    ).astype(jnp.bfloat16)
    gate_full, up_full = (
        lax.all_gather(w_gate, "req", axis=0, tiled=True),
        lax.all_gather(w_up, "req", axis=0, tiled=True),
    )
    down_full = lax.all_gather(w_down, "req", axis=1, tiled=True)
    shard_rows = lax.all_gather(normed, "seq", axis=0, tiled=True)
    gate_part = jnp.dot(shard_rows, gate_full, preferred_element_type=jnp.float32)
    upward = jnp.dot(shard_rows, up_full, preferred_element_type=jnp.float32)
    inner_units = (jax.nn.silu(gate_part) * upward).astype(jnp.bfloat16)
    summed = lax.psum_scatter(
        jnp.dot(inner_units, down_full, preferred_element_type=jnp.float32).astype(jnp.bfloat16),
        "seq",
        scatter_dimension=0,
        tiled=True,
    ).astype(jnp.float32)
    combined = stream + summed
    hidden_out = jnp.where(live_mask[:, None], combined, 0.0).astype(jnp.bfloat16)
    return (hidden_out[None], state_part[None], edge_part.astype(jnp.bfloat16)[None])


def solution(mesh):
    return jax.shard_map(
        local,
        mesh=mesh,
        in_specs=(
            P("req", "seq", None),
            P("req", "seq", None),
            P("req", "seq", None),
            P("req", "seq", None),
            P("req", "seq", None),
            P(),
            P(),
            P(),
            P(),
            P(("req", "seq"), None),
            P(),
            P("req", "seq"),
            P("req", "seq"),
            P("seq", "req"),
        ),
        out_specs=(P("req", "seq", None), P("req", "seq", None, None), P("req", None, "seq")),
        check_vma=False,
    )
```

profile of v0, /device:TPU:0, one launch (start us, length us, event | category | flops | bytes accessed | tf_op | source)
XLA Modules:
  0.0 511.9 jit_solution(8159952312244182873)
XLA Ops:
  12.3 1.9 fusion.106
  17.2 3.4 divide_multiply_fusion
  20.6 1.4 multiply_bitcast_fusion
  23.9 1.8 fusion.72
  25.7 80.0 %custom-call.3 = f32[8,2,1,64,64]{3,4,2,1,0:T(8,128)} custom-call(f32[8,2,1,64,64]{4,3,2,1,0:T(8,128)} %fusion.72), custom_call_target="InvertDiagBlocksLowerTriangular" | custom-call | tf_op jit(solution)/shard_map/triangular_solve | solution.py:45
  105.7 2.0 fusion.85
  107.8 1.7 convolution_bitcast_fusion.2
  111.8 4.1 while.90
  116.8 5.9 %collective-permute-start.1 = (bf16[8,128,256]{2,1,0:T(8,128)(2,1)}, bf16[8,128,256]{2,1,0:T(8,128)(2,1)}, u32[]{:S(2)}, u32[]{:S(2)}) collective-permute-start(bf16[8,128,256]{2,1,0:T(8,128)(2,1)} %convert_element_type.129), channel_id=1, source_target_pairs={{0,1},{1,2},{2,3},{3,4},{4,5},{5,6},{6,7},{8,9},{9,10},{10,11},{11... | collective-permute-start | bytes 1572872 | tf_op jit(solution)/shard_map/ppermute | solution.py:20
  124.5 4.2 while.83
  125.3 1.3 convolution_add_fusion.18
  127.4 1.3 convolution_add_fusion.18
  129.6 7.3 %collective-permute-start.2 = (bf16[8,128,256]{2,1,0:T(8,128)(2,1)}, bf16[8,128,256]{2,1,0:T(8,128)(2,1)}, u32[]{:S(2)}, u32[]{:S(2)}) collective-permute-start(bf16[8,128,256]{2,1,0:T(8,128)(2,1)} %convert_element_type.131), channel_id=1, source_target_pairs={{0,1},{1,2},{2,3},{3,4},{4,5},{5,6},{6,7},{8,9},{9,10},{10,11},{11... | collective-permute-start | bytes 1572872 | tf_op jit(solution)/shard_map/ppermute | solution.py:20
  139.1 4.2 while.84
  139.8 1.3 convolution_add_fusion.19
  144.2 9.7 %collective-permute-start.3 = (bf16[8,128,256]{2,1,0:T(8,128)(2,1)}, bf16[8,128,256]{2,1,0:T(8,128)(2,1)}, u32[]{:S(2)}, u32[]{:S(2)}) collective-permute-start(bf16[8,128,256]{2,1,0:T(8,128)(2,1)} %convert_element_type.133), channel_id=1, source_target_pairs={{0,1},{1,2},{2,3},{3,4},{4,5},{5,6},{6,7},{8,9},{9,10},{10,11},{11... | collective-permute-start | bytes 1572872 | tf_op jit(solution)/shard_map/ppermute | solution.py:20
  156.1 4.2 while.85
  161.2 9.7 %collective-permute-start.4 = (bf16[8,128,256]{2,1,0:T(8,128)(2,1)}, bf16[8,128,256]{2,1,0:T(8,128)(2,1)}, u32[]{:S(2)}, u32[]{:S(2)}) collective-permute-start(bf16[8,128,256]{2,1,0:T(8,128)(2,1)} %convert_element_type.135), channel_id=1, source_target_pairs={{0,1},{1,2},{2,3},{3,4},{4,5},{5,6},{6,7},{8,9},{9,10},{10,11},{11... | collective-permute-start | bytes 1572872 | tf_op jit(solution)/shard_map/ppermute | solution.py:20
  173.2 4.2 while.86
  178.3 9.7 %collective-permute-start.5 = (bf16[8,128,256]{2,1,0:T(8,128)(2,1)}, bf16[8,128,256]{2,1,0:T(8,128)(2,1)}, u32[]{:S(2)}, u32[]{:S(2)}) collective-permute-start(bf16[8,128,256]{2,1,0:T(8,128)(2,1)} %convert_element_type.137), channel_id=1, source_target_pairs={{0,1},{1,2},{2,3},{3,4},{4,5},{5,6},{6,7},{8,9},{9,10},{10,11},{11... | collective-permute-start | bytes 1572872 | tf_op jit(solution)/shard_map/ppermute | solution.py:20
  190.2 4.2 while.87
  195.2 9.7 %collective-permute-start.6 = (bf16[8,128,256]{2,1,0:T(8,128)(2,1)}, bf16[8,128,256]{2,1,0:T(8,128)(2,1)}, u32[]{:S(2)}, u32[]{:S(2)}) collective-permute-start(bf16[8,128,256]{2,1,0:T(8,128)(2,1)} %convert_element_type.139), channel_id=1, source_target_pairs={{0,1},{1,2},{2,3},{3,4},{4,5},{5,6},{6,7},{8,9},{9,10},{10,11},{11... | collective-permute-start | bytes 1572872 | tf_op jit(solution)/shard_map/ppermute | solution.py:20
  206.9 1.9 copy.258
  210.0 4.2 while.88
  210.7 1.3 convolution_add_fusion.23
  212.8 1.3 convolution_add_fusion.23
  214.2 6.3 %collective-permute-start.7 = (bf16[8,128,256]{2,1,0:T(8,128)(2,1)S(1)}, bf16[8,128,256]{2,1,0:T(8,128)(2,1)S(1)}, u32[]{:S(2)}, u32[]{:S(2)}) collective-permute-start(bf16[8,128,256]{2,1,0:T(8,128)(2,1)S(1)} %convert_element_type.141), channel_id=1, source_target_pairs={{0,1},{1,2},{2,3},{3,4},{4,5},{5,6},{6,7},{8,9},{9,10},{10,11},{11... | collective-permute-start | bytes 1572872 | tf_op jit(solution)/shard_map/ppermute | solution.py:20
  222.9 1.9 fusion.70
  224.9 10.8 %while.89 = (s32[]{:T(128)}, f32[8,128,256]{2,1,0:T(8,128)S(1)}, f32[2,8,64,256]{3,2,1,0:T(8,128)}, f32[2,8]{1,0:T(2,128)S(1)}, f32[2,8,64,128]{3,2,1,0:T(8,128)...) while((s32[]{:T(128)}, f32[8,128,256]{2,1,0:T(8,128)S(1)}, ...), condition=%wide.region_20.21_spmd, body=%wide.region_19.20_spmd.sunk | while | flops 705429504 | bytes 19925256 | solution.py:85
  225.7 1.5 fusion.223
  231.1 1.5 fusion.223
  235.8 1.5 multiply_reduce_fusion.1
  237.6 1.4 copy.261
  239.6 1.3 copy.260
  241.0 5.8 %multiply_reduce_fusion = (f32[128]{0:T(128)S(1)}, f32[128,2048]{1,0:T(8,128)S(1)}) fusion(bf16[2048,2048]{1,0:T(8,128)(2,1)} %all-gather.6.cloned.1.call-done, f32[128,2048]{1,0:T(8,128)} %bitcast.348, f32[128,2048]{1,0:T(8,128)} %bitcast.347, bf16[1,128,2048]{2,1,0:T(8,128)(2,1)} %param.31, f32[2048]{0:T(1024)S(1)} %bitcast.360, ...), kind=kOutput, calls=%fused_computation.125 | convolution fusion | flops 1077673856 | bytes 12591616 | tf_op jit(solution)/shard_map/dot_general | solution.py:158
  249.9 1.4 copy.250
  252.6 6.2 %all-gather.10.cloned.1.call-done = bf16[2048,704]{0,1:T(8,128)(2,1)} async-done(((bf16[128,704]{0,1:T(8,128)(2,1)}), bf16[2048,704]{0,1:T(8,128)(2,1)}) %all-gather.10.cloned.1.call-update) | async-done | bytes 2883600 | tf_op jit(solution)/shard_map/all_gather | solution.py:169
  258.8 34.0 %all-gather.8.cloned.1.call-done = bf16[1024,2048]{1,0:T(8,128)(2,1)} async-done(((bf16[128,2048]{1,0:T(8,128)(2,1)}), bf16[1024,2048]{1,0:T(8,128)(2,1)}) %all-gather.8.cloned.1.call-update) | async-done | bytes 4194320 | tf_op jit(solution)/shard_map/all_gather | solution.py:173
  292.8 7.8 %fusion.114 = f32[1024,704]{0,1:T(8,128)} fusion(bf16[1024,2048]{1,0:T(8,128)(2,1)} %all-gather.8.cloned.1.call-done, bf16[2048,704]{0,1:T(8,128)(2,1)} %all-gather.10.cloned.1.call-done), kind=kOutput, calls=%fused_computation.195 | convolution fusion | flops 2952790016 | bytes 9961472 | tf_op jit(solution)/shard_map/dot_general | solution.py:174
  300.7 44.4 %all-gather.12.cloned.1.call-done = bf16[2048,704]{0,1:T(8,128)(2,1)} async-done(((bf16[128,704]{0,1:T(8,128)(2,1)}), bf16[2048,704]{0,1:T(8,128)(2,1)}) %all-gather.12.cloned.1.call-update) | async-done | bytes 2883600 | tf_op jit(solution)/shard_map/all_gather | solution.py:170
  345.1 51.8 %all-gather.14.cloned.1.call-done = bf16[704,2048]{1,0:T(8,128)(2,1)} async-done(((bf16[704,128]{1,0:T(8,128)(2,1)}), bf16[704,2048]{1,0:T(8,128)(2,1)}) %all-gather.14.cloned.1.call-update) | async-done | bytes 2883600 | tf_op jit(solution)/shard_map/all_gather | solution.py:172
  396.9 12.0 %convolution_convert_fusion.1 = bf16[1024,2048]{1,0:T(8,128)(2,1)} fusion(bf16[704,2048]{1,0:T(8,128)(2,1)} %all-gather.14.cloned.1.call-done, f32[1024,704]{0,1:T(8,128)} %fusion.114, bf16[1024,2048]{1,0:T(8,128)(2,1)} %all-gather.8.cloned.1.call-done, bf16[2048,704]{0,1:T(8,128)(2,1)} %all-gather.12.cloned.1.call-done), kind=kOutput, calls=%fused_computation.94 | convolution fusion | flops 5912002560 | bytes 17039360 | tf_op jit(solution)/shard_map/dot_general | solution.py:178
  409.5 21.5 %reduce-scatter.10.cloned.1.call-done = bf16[512,3]{1,0:T(8,128)(2,1)} async-done(((bf16[4096,3]{1,0:T(8,128)(2,1)}), bf16[512,3]{1,0:T(8,128)(2,1)}) %reduce-scatter.10.cloned.1.call-update) | async-done | bytes 3088
  431.0 1.6 copy.251
  432.6 31.0 %reduce-scatter.8.cloned.1.call-done = bf16[1,128,256]{2,1,0:T(8,128)(2,1)} async-done(((bf16[8,128,256]{2,1,0:T(8,128)(2,1)}), bf16[1,128,256]{2,1,0:T(8,128)(2,1)}) %reduce-scatter.8.cloned.1.call-update) | async-done | bytes 65552 | tf_op jit(solution)/shard_map/reduce_scatter | solution.py:144
  463.6 1.5 bitcast_convert_fusion
  465.1 37.8 %reduce-scatter.6.cloned.1.call-done = bf16[128,2048]{1,0:T(8,128)(2,1)} async-done(((bf16[1024,2048]{1,0:T(8,128)(2,1)}), bf16[128,2048]{1,0:T(8,128)(2,1)}) %reduce-scatter.6.cloned.1.call-update) | async-done | bytes 524304 | tf_op jit(solution)/shard_map/reduce_scatter | solution.py:177
  502.9 2.0 fusion.82
  (177 shorter events, 68.4 us)
Async XLA Ops:
  7.2 198.2 %copy-start = (f32[256]{0:T(256)S(1)}, f32[256]{0:T(256)}, u32[]{:S(2)}) copy-start(f32[256]{0:T(256)} %param.38) | copy-start | bytes 3076
  7.2 233.8 %all-gather.6.cloned.1.call-start = ((), (), s32[]{:S(2)}) async-start(), calls=%async_computation.3 | async-start | bytes 8454144 | tf_op jit(solution)/shard_map/all_gather | solution.py:160
  8.1 9.1 %collective-permute-start = (bf16[3,4096]{1,0:T(4,128)(2,1)S(1)}, bf16[3,4096]{1,0:T(4,128)(2,1)S(1)}, u32[]{:S(2)}, u32[]{:S(2)}) collective-permute-start(bf16[3,4096]{1,0:T(4,128)(2,1)S(1)} %slice_bitcast_fusion.2), channel_id=1, source_target_pairs={{0,1},{1,2},{2,3},{3,4},{4,5},{5,6},{6,7},{8,9},{9,10},{10,11},{11... | collective-permute-start | bytes 73736 | tf_op jit(solution)/shard_map/ppermute | solution.py:20
  9.4 249.4 %all-gather.10.cloned.1.call-start = ((), (), s32[]{:S(2)}) async-start(), calls=%async_computation.5 | async-start | bytes 3063808 | tf_op jit(solution)/shard_map/all_gather | solution.py:169
  20.6 1.7 copy-start.2
  23.9 83.9 %copy-start.9 = (f32[8,2,64,128]{3,0,2,1:T(8,128)}, f32[8,2,64,128]{3,0,2,1:T(8,128)S(1)}, u32[]{:S(2)}) copy-start(f32[8,2,64,128]{3,0,2,1:T(8,128)S(1)} %get-tuple-element.663) | copy-start | bytes 1572868
  23.9 85.7 %slice-start = ((f32[128,4096]{1,0:T(8,128)}), f32[128,2048]{1,0:T(8,128)S(1)}, s32[]{:S(2)}) async-start(f32[128,4096]{1,0:T(8,128)} %copy-done.2), calls=%async_computation.11 | async-start | bytes 2097152 | tf_op jit(solution)/shard_map/slice | solution.py:125
  116.8 6.6 %collective-permute-start.1 = (bf16[8,128,256]{2,1,0:T(8,128)(2,1)}, bf16[8,128,256]{2,1,0:T(8,128)(2,1)}, u32[]{:S(2)}, u32[]{:S(2)}) collective-permute-start(bf16[8,128,256]{2,1,0:T(8,128)(2,1)} %convert_element_type.129), channel_id=1, source_target_pairs={{0,1},{1,2},{2,3},{3,4},{4,5},{5,6},{6,7},{8,9},{9,10},{10,11},{11... | collective-permute-start | bytes 1572872 | tf_op jit(solution)/shard_map/ppermute | solution.py:20
  129.6 8.3 %collective-permute-start.2 = (bf16[8,128,256]{2,1,0:T(8,128)(2,1)}, bf16[8,128,256]{2,1,0:T(8,128)(2,1)}, u32[]{:S(2)}, u32[]{:S(2)}) collective-permute-start(bf16[8,128,256]{2,1,0:T(8,128)(2,1)} %convert_element_type.131), channel_id=1, source_target_pairs={{0,1},{1,2},{2,3},{3,4},{4,5},{5,6},{6,7},{8,9},{9,10},{10,11},{11... | collective-permute-start | bytes 1572872 | tf_op jit(solution)/shard_map/ppermute | solution.py:20
  144.2 10.8 %collective-permute-start.3 = (bf16[8,128,256]{2,1,0:T(8,128)(2,1)}, bf16[8,128,256]{2,1,0:T(8,128)(2,1)}, u32[]{:S(2)}, u32[]{:S(2)}) collective-permute-start(bf16[8,128,256]{2,1,0:T(8,128)(2,1)} %convert_element_type.133), channel_id=1, source_target_pairs={{0,1},{1,2},{2,3},{3,4},{4,5},{5,6},{6,7},{8,9},{9,10},{10,11},{11... | collective-permute-start | bytes 1572872 | tf_op jit(solution)/shard_map/ppermute | solution.py:20
  161.2 10.8 %collective-permute-start.4 = (bf16[8,128,256]{2,1,0:T(8,128)(2,1)}, bf16[8,128,256]{2,1,0:T(8,128)(2,1)}, u32[]{:S(2)}, u32[]{:S(2)}) collective-permute-start(bf16[8,128,256]{2,1,0:T(8,128)(2,1)} %convert_element_type.135), channel_id=1, source_target_pairs={{0,1},{1,2},{2,3},{3,4},{4,5},{5,6},{6,7},{8,9},{9,10},{10,11},{11... | collective-permute-start | bytes 1572872 | tf_op jit(solution)/shard_map/ppermute | solution.py:20
  178.3 10.8 %collective-permute-start.5 = (bf16[8,128,256]{2,1,0:T(8,128)(2,1)}, bf16[8,128,256]{2,1,0:T(8,128)(2,1)}, u32[]{:S(2)}, u32[]{:S(2)}) collective-permute-start(bf16[8,128,256]{2,1,0:T(8,128)(2,1)} %convert_element_type.137), channel_id=1, source_target_pairs={{0,1},{1,2},{2,3},{3,4},{4,5},{5,6},{6,7},{8,9},{9,10},{10,11},{11... | collective-permute-start | bytes 1572872 | tf_op jit(solution)/shard_map/ppermute | solution.py:20
  195.2 13.6 %collective-permute-start.6 = (bf16[8,128,256]{2,1,0:T(8,128)(2,1)}, bf16[8,128,256]{2,1,0:T(8,128)(2,1)}, u32[]{:S(2)}, u32[]{:S(2)}) collective-permute-start(bf16[8,128,256]{2,1,0:T(8,128)(2,1)} %convert_element_type.139), channel_id=1, source_target_pairs={{0,1},{1,2},{2,3},{3,4},{4,5},{5,6},{6,7},{8,9},{9,10},{10,11},{11... | collective-permute-start | bytes 1572872 | tf_op jit(solution)/shard_map/ppermute | solution.py:20
  205.0 87.8 %all-gather.8.cloned.1.call-start = ((), (), s32[]{:S(2)}) async-start(), calls=%async_computation.4 | async-start | bytes 4718592 | tf_op jit(solution)/shard_map/all_gather | solution.py:173
  214.2 7.6 %copy-start.4 = (f32[16,8,8,128]{3,2,1,0:T(8,128)S(1)}, f32[16,8,8,128]{3,2,1,0:T(8,128)}, u32[]{:S(2)}) copy-start(f32[16,8,8,128]{3,2,1,0:T(8,128)} %copy.258) | copy-start | bytes 1572868
  214.2 8.8 %copy-start.10 = (f32[8,2,64,128]{3,0,2,1:T(8,128)S(1)}, f32[8,2,64,128]{3,0,2,1:T(8,128)}, u32[]{:S(2)}) copy-start(f32[8,2,64,128]{3,0,2,1:T(8,128)} %copy-done.9) | copy-start | bytes 1572868
  214.2 10.6 %collective-permute-start.7 = (bf16[8,128,256]{2,1,0:T(8,128)(2,1)S(1)}, bf16[8,128,256]{2,1,0:T(8,128)(2,1)S(1)}, u32[]{:S(2)}, u32[]{:S(2)}) collective-permute-start(bf16[8,128,256]{2,1,0:T(8,128)(2,1)S(1)} %convert_element_type.141), channel_id=1, source_target_pairs={{0,1},{1,2},{2,3},{3,4},{4,5},{5,6},{6,7},{8,9},{9,10},{10,11},{11... | collective-permute-start | bytes 1572872 | tf_op jit(solution)/shard_map/ppermute | solution.py:20
  224.9 2.3 copy-start.3
  225.0 2.3 copy-start.6
  228.0 1.0 copy-start.7
  230.4 2.3 copy-start.3
  230.4 2.3 copy-start.6
  233.4 1.0 copy-start.7
  235.8 3.3 copy-start.8
  241.0 5.8 %copy-start.11 = (f32[2048]{0:T(1024)S(1)}, f32[2048]{0:T(1024)}, u32[]{:S(2)}) copy-start(f32[2048]{0:T(1024)} %param.40) | copy-start | bytes 24580
  241.0 8.6 %copy-start.5 = (bf16[1,128,4096]{2,1,0:T(8,128)(2,1)S(1)}, bf16[1,128,4096]{2,1,0:T(8,128)(2,1)}, u32[]{:S(2)}) copy-start(bf16[1,128,4096]{2,1,0:T(8,128)(2,1)} %param.30) | copy-start | bytes 3145732
  247.8 97.3 %all-gather.12.cloned.1.call-start = ((), (), s32[]{:S(2)}) async-start(), calls=%async_computation.6 | async-start | bytes 3063808 | tf_op jit(solution)/shard_map/all_gather | solution.py:170
  248.4 148.5 %all-gather.14.cloned.1.call-start = ((), (), s32[]{:S(2)}) async-start(), calls=%async_computation.7 | async-start | bytes 3063808 | tf_op jit(solution)/shard_map/all_gather | solution.py:172
  249.0 182.0 %reduce-scatter.10.cloned.1.call-start = ((), (), s32[]{:S(2)}) async-start(), calls=%async_computation.10 | async-start | bytes 1179648
  251.3 212.2 %reduce-scatter.8.cloned.1.call-start = ((), (), s32[]{:S(2)}) async-start(), calls=%async_computation.9 | async-start | bytes 589824 | tf_op jit(solution)/shard_map/reduce_scatter | solution.py:144
  252.3 250.5 %reduce-scatter.6.cloned.1.call-start = ((), (), s32[]{:S(2)}) async-start(), calls=%async_computation.8 | async-start | bytes 4718592 | tf_op jit(solution)/shard_map/reduce_scatter | solution.py:177
  408.9 96.0 %copy-start.1 = (f32[256]{0:T(256)S(1)}, f32[256]{0:T(256)}, u32[]{:S(2)}) copy-start(f32[256]{0:T(256)} %param.38) | copy-start | bytes 3076
Sparse Core Ops, SparseCore 0:
  11.0 74.0 all-gather.5
  205.1 53.6 all-gather.9
  261.1 31.6 all-gather.7
  294.8 50.2 all-gather.11
  347.0 49.8 all-gather.13
  399.2 31.8 reduce-scatter.9
  433.4 30.1 reduce-scatter.7
  466.0 36.8 reduce-scatter.5
where the time goes:
time: 521 us; the launch traced here: 512 us
  waiting for transfers between devices  233 us (45%)
  other arithmetic  114 us (22%)
  matrix products  71.7 us (14%)
  starting transfers between devices  60.5 us (12%)
  local copies, waits for them, and re-layouts  16.5 us (3%)
  between operations  15.4 us (3%)
    another operation x4, other arithmetic, block_tables(): lax.linalg.triangular_solve(identity + couple, identity, left_side=True,...  80.1 us
    ppermute x8, starting transfers between devices, shifted(): lax.ppermute(value, axis, [(source, source + steps) for source in range(i...  59.8 us
    all_gather x1, waiting for transfers between devices, local(): down_full = lax.all_gather(w_down, 'req', axis=1, tiled=True)  51.8 us
    all_gather x1, waiting for transfers between devices, local(): lax.all_gather(w_up, 'req', axis=0, tiled=True)  44.4 us
    reduce_scatter x1, waiting for transfers between devices, local(): lax.psum_scatter(jnp.dot(inner_units, down_full, preferred_element_type=j...  37.8 us
    all_gather x1, waiting for transfers between devices, local(): shard_rows = lax.all_gather(normed, 'seq', axis=0, tiled=True)  34 us
    reduce_scatter x1, waiting for transfers between devices, local(): lax.psum_scatter(state_term.astype(jnp.bfloat16), 'seq', scatter_dimensio...  31 us
    unnamed x9, waiting for transfers between devices  22.7 us
  transfers between devices with their start and end apart: 16, of which 12 were waited for; matrix products, arithmetic and copies ran while one was open for 39% of the time, Pallas kernels for 0%

commit v1 on v0

--- a/solution.py
+++ b/solution.py
@@ -12,6 +12,28 @@
 EPS_NORM = 1e-05
 EPS_UNIT = 1e-06
 HIGHEST = lax.Precision.HIGHEST
+
+
+def joined_along(parts, dim):
+    shape = list(parts.shape[1:])
+    shape[dim] *= parts.shape[0]
+    return jnp.moveaxis(parts, 0, dim).reshape(shape)
+
+
+def collect(shard, axis, dim):
+    peers = lax.axis_size(axis)
+    pairs = [(i, (i + 1) % peers) for i in range(peers)]
+    back = [(b, a) for a, b in pairs]
+    lower, upper = ([], [])
+    for lap in range(peers - 1):
+        if lap % 2 == 0:
+            lower.append(lax.ppermute(lower[-1] if lower else shard, axis, pairs))
+        else:
+            upper.append(lax.ppermute(upper[-1] if upper else shard, axis, back))
+    blocks = jnp.stack([*lower[::-1], shard, *upper])
+    shift = lax.axis_index(axis) - len(lower)
+    blocks = blocks[(jnp.arange(peers) - shift) % peers]
+    return joined_along(blocks, dim)
 
 
 def shifted(value, axis, steps):
@@ -167,7 +189,7 @@
     ).astype(jnp.bfloat16)
     gate_full, up_full = (
         lax.all_gather(w_gate, "req", axis=0, tiled=True),
-        lax.all_gather(w_up, "req", axis=0, tiled=True),
+        collect(w_up, "req", 0),
     )
     down_full = lax.all_gather(w_down, "req", axis=1, tiled=True)
     shard_rows = lax.all_gather(normed, "seq", axis=0, tiled=True)

time: 521 us -> 472 us (0.906)
  waiting for transfers between devices: 233 us -> 119 us
  starting transfers between devices: 60.5 us -> 102 us
  local copies, waits for them, and re-layouts: 16.5 us -> 40 us
    all_gather x1, waiting for transfers between devices: 51.8 us -> 0.01 us  [local(): down_full = lax.all_gather(w_down, 'req', axis=1, tiled=True)]
    all_gather x1 -> x0, waiting for transfers between devices: 44.4 us -> none  [local(): lax.all_gather(w_up, 'req', axis=0, tiled=True)]
    ppermute x0 -> x15, starting transfers between devices: none -> 41.6 us  [the longest x7 40 us: collect(): upper.append(lax.ppermute(upper[-1] if upper else shard, axis, back))]
    all_gather x1, waiting for transfers between devices: 34 us -> 0.02 us  [local(): shard_rows = lax.all_gather(normed, 'seq', axis=0, tiled=True)]
    ppermute x0 -> x15, waiting for transfers between devices: none -> 33.5 us  [the longest x8 31.1 us: collect(): lower.append(lax.ppermute(lower[-1] if lower else shard, axis, pairs))]
    unnamed x32 -> x61, local copies, waits for them, and re-layouts: 9.73 us -> 28.2 us
    unnamed x9 -> x8, waiting for transfers between devices: 22.7 us -> 12.1 us
    all_gather x1, waiting for transfers between devices: 6.25 us -> 0.02 us  [local(): lax.all_gather(w_gate, 'req', axis=0, tiled=True)]
  transfers between devices with their start and end apart: 16 -> 30, of which waited for: 12 -> 21; matrix products, arithmetic and copies ran while one was open for 39% -> 48% of each run, Pallas kernels for 0% -> 0%
where the time goes in v1:
time: 472 us; the launch traced here: 464 us
  waiting for transfers between devices  119 us (25%)
  other arithmetic  114 us (24%)
  starting transfers between devices  102 us (22%)
  matrix products  71.9 us (15%)
  local copies, waits for them, and re-layouts  40 us (8%)
  between operations  15.7 us (3%)
    another operation x4, other arithmetic, block_tables(): lax.linalg.triangular_solve(identity + couple, identity, left_side=True,...  80.1 us
    ppermute x8, starting transfers between devices, shifted(): lax.ppermute(value, axis, [(source, source + steps) for source in range(i...  59.8 us
    ppermute x7, starting transfers between devices, collect(): upper.append(lax.ppermute(upper[-1] if upper else shard, axis, back))  40 us
    reduce_scatter x1, waiting for transfers between devices, local(): lax.psum_scatter(jnp.dot(inner_units, down_full, preferred_element_type=j...  37.7 us
    ppermute x8, waiting for transfers between devices, collect(): lower.append(lax.ppermute(lower[-1] if lower else shard, axis, pairs))  31.1 us
    reduce_scatter x1, waiting for transfers between devices, local(): lax.psum_scatter(state_term.astype(jnp.bfloat16), 'seq', scatter_dimensio...  30.8 us
    unnamed x61, local copies, waits for them, and re-layouts  28.2 us
    dot_general x16, matrix products, advance(): jnp.einsum('hck,hcx->hkx', keys_now, corrected, precision=HIGHEST)  21.1 us
  transfers between devices with their start and end apart: 30, of which 21 were waited for; matrix products, arithmetic and copies ran while one was open for 48% of the time, Pallas kernels for 0%

profile of v1, /device:TPU:0, one launch (start us, length us, event | category | flops | bytes accessed | tf_op | source)
XLA Modules:
  0.0 463.5 jit_solution(18137890377478582229)
XLA Ops:
  12.3 2.0 fusion.113
  17.4 3.5 divide_multiply_fusion
  24.1 1.8 fusion.77
  25.9 80.0 %custom-call.3 = f32[8,2,1,64,64]{3,4,2,1,0:T(8,128)} custom-call(f32[8,2,1,64,64]{4,3,2,1,0:T(8,128)} %fusion.77), custom_call_target="InvertDiagBlocksLowerTriangular" | custom-call | tf_op jit(solution)/shard_map/triangular_solve | solution.py:67
  105.9 2.0 fusion.92
  108.0 1.7 convolution_bitcast_fusion.2
  112.0 4.1 while.90
  117.0 6.0 %collective-permute-start.1 = (bf16[8,128,256]{2,1,0:T(8,128)(2,1)}, bf16[8,128,256]{2,1,0:T(8,128)(2,1)}, u32[]{:S(2)}, u32[]{:S(2)}) collective-permute-start(bf16[8,128,256]{2,1,0:T(8,128)(2,1)} %convert_element_type.129), channel_id=1, source_target_pairs={{0,1},{1,2},{2,3},{3,4},{4,5},{5,6},{6,7},{8,9},{9,10},{10,11},{11... | collective-permute-start | bytes 1572872 | tf_op jit(solution)/shard_map/ppermute | solution.py:42
  124.7 4.2 while.83
  129.7 7.3 %collective-permute-start.2 = (bf16[8,128,256]{2,1,0:T(8,128)(2,1)}, bf16[8,128,256]{2,1,0:T(8,128)(2,1)}, u32[]{:S(2)}, u32[]{:S(2)}) collective-permute-start(bf16[8,128,256]{2,1,0:T(8,128)(2,1)} %convert_element_type.131), channel_id=1, source_target_pairs={{0,1},{1,2},{2,3},{3,4},{4,5},{5,6},{6,7},{8,9},{9,10},{10,11},{11... | collective-permute-start | bytes 1572872 | tf_op jit(solution)/shard_map/ppermute | solution.py:42
  139.2 4.2 while.84
  144.2 9.7 %collective-permute-start.3 = (bf16[8,128,256]{2,1,0:T(8,128)(2,1)}, bf16[8,128,256]{2,1,0:T(8,128)(2,1)}, u32[]{:S(2)}, u32[]{:S(2)}) collective-permute-start(bf16[8,128,256]{2,1,0:T(8,128)(2,1)} %convert_element_type.133), channel_id=1, source_target_pairs={{0,1},{1,2},{2,3},{3,4},{4,5},{5,6},{6,7},{8,9},{9,10},{10,11},{11... | collective-permute-start | bytes 1572872 | tf_op jit(solution)/shard_map/ppermute | solution.py:42
  156.2 4.2 while.85
  161.2 9.7 %collective-permute-start.4 = (bf16[8,128,256]{2,1,0:T(8,128)(2,1)}, bf16[8,128,256]{2,1,0:T(8,128)(2,1)}, u32[]{:S(2)}, u32[]{:S(2)}) collective-permute-start(bf16[8,128,256]{2,1,0:T(8,128)(2,1)} %convert_element_type.135), channel_id=1, source_target_pairs={{0,1},{1,2},{2,3},{3,4},{4,5},{5,6},{6,7},{8,9},{9,10},{10,11},{11... | collective-permute-start | bytes 1572872 | tf_op jit(solution)/shard_map/ppermute | solution.py:42
  173.1 4.2 while.86
  178.2 9.8 %collective-permute-start.5 = (bf16[8,128,256]{2,1,0:T(8,128)(2,1)}, bf16[8,128,256]{2,1,0:T(8,128)(2,1)}, u32[]{:S(2)}, u32[]{:S(2)}) collective-permute-start(bf16[8,128,256]{2,1,0:T(8,128)(2,1)} %convert_element_type.137), channel_id=1, source_target_pairs={{0,1},{1,2},{2,3},{3,4},{4,5},{5,6},{6,7},{8,9},{9,10},{10,11},{11... | collective-permute-start | bytes 1572872 | tf_op jit(solution)/shard_map/ppermute | solution.py:42
  190.1 4.2 while.87
  195.1 9.8 %collective-permute-start.6 = (bf16[8,128,256]{2,1,0:T(8,128)(2,1)}, bf16[8,128,256]{2,1,0:T(8,128)(2,1)}, u32[]{:S(2)}, u32[]{:S(2)}) collective-permute-start(bf16[8,128,256]{2,1,0:T(8,128)(2,1)} %convert_element_type.139), channel_id=1, source_target_pairs={{0,1},{1,2},{2,3},{3,4},{4,5},{5,6},{6,7},{8,9},{9,10},{10,11},{11... | collective-permute-start | bytes 1572872 | tf_op jit(solution)/shard_map/ppermute | solution.py:42
  206.9 1.9 copy.263
  209.9 4.2 while.88
  214.2 6.3 %collective-permute-start.7 = (bf16[8,128,256]{2,1,0:T(8,128)(2,1)S(1)}, bf16[8,128,256]{2,1,0:T(8,128)(2,1)S(1)}, u32[]{:S(2)}, u32[]{:S(2)}) collective-permute-start(bf16[8,128,256]{2,1,0:T(8,128)(2,1)S(1)} %convert_element_type.141), channel_id=1, source_target_pairs={{0,1},{1,2},{2,3},{3,4},{4,5},{5,6},{6,7},{8,9},{9,10},{10,11},{11... | collective-permute-start | bytes 1572872 | tf_op jit(solution)/shard_map/ppermute | solution.py:42
  222.9 1.9 fusion.75
  224.9 10.8 %while.89 = (s32[]{:T(128)}, f32[8,128,256]{2,1,0:T(8,128)S(1)}, f32[2,8,64,256]{3,2,1,0:T(8,128)}, f32[2,8]{1,0:T(2,128)S(1)}, f32[2,8,64,128]{3,2,1,0:T(8,128)...) while((s32[]{:T(128)}, f32[8,128,256]{2,1,0:T(8,128)S(1)}, ...), condition=%wide.region_20.21_spmd, body=%wide.region_19.20_spmd.sunk | while | flops 705429504 | bytes 19925256 | solution.py:107
  240.9 5.8 %multiply_reduce_fusion = (f32[128]{0:T(128)S(1)}, f32[128,2048]{1,0:T(8,128)S(1)}) fusion(bf16[2048,2048]{1,0:T(8,128)(2,1)} %all-gather.5.cloned.1.call-done, f32[128,2048]{1,0:T(8,128)} %bitcast.393, f32[128,2048]{1,0:T(8,128)} %bitcast.392, bf16[1,128,2048]{2,1,0:T(8,128)(2,1)} %param.31, f32[2048]{0:T(1024)S(1)} %bitcast.405, ...), kind=kOutput, calls=%fused_computation.129 | convolution fusion | flops 1077673856 | bytes 12591616 | tf_op jit(solution)/shard_map/dot_general | solution.py:180
  249.9 8.1 %collective-permute-done.8 = bf16[128,704]{0,1:T(8,128)(2,1)S(1)} collective-permute-done((bf16[128,704]{0,1:T(8,128)(2,1)S(1)}, bf16[128,704]{0,1:T(8,128)(2,1)S(1)}, u32[]{:S(2)}, u32[]{:S(2)}) %collective-permute-start.8) | collective-permute-done | bytes 180256 | tf_op jit(solution)/shard_map/ppermute | solution.py:30
  258.1 5.5 %collective-permute-start.16 = (bf16[128,704]{0,1:T(8,128)(2,1)S(1)}, bf16[128,704]{0,1:T(8,128)(2,1)S(1)}, u32[]{:S(2)}, u32[]{:S(2)}) collective-permute-start(bf16[128,704]{0,1:T(8,128)(2,1)S(1)} %copy-done.11), channel_id=1, source_target_pairs={{8,0},{16,8},{24,16},{32,24},{40,32},{48,40},{56,48},{64,56},{72,6... | collective-permute-start | bytes 540680 | tf_op jit(solution)/shard_map/ppermute | solution.py:32
  263.6 3.3 collective-permute-done.9
  267.6 5.5 %collective-permute-start.17 = (bf16[128,704]{0,1:T(8,128)(2,1)S(1)}, bf16[128,704]{0,1:T(8,128)(2,1)}, u32[]{:S(2)}, u32[]{:S(2)}) collective-permute-start(bf16[128,704]{0,1:T(8,128)(2,1)S(1)} %collective-permute-done.16), channel_id=1, source_target_pairs={{8,0},{16,8},{24,16},{32,24},{40,32},{48,40},{56,48},{64,56},{72,6... | collective-permute-start | bytes 540680 | tf_op jit(solution)/shard_map/ppermute | solution.py:32
  273.1 2.6 collective-permute-done.10
  276.1 5.9 %collective-permute-start.18 = (bf16[128,704]{0,1:T(8,128)(2,1)}, bf16[128,704]{0,1:T(8,128)(2,1)}, u32[]{:S(2)}, u32[]{:S(2)}) collective-permute-start(bf16[128,704]{0,1:T(8,128)(2,1)} %collective-permute-done.17), channel_id=1, source_target_pairs={{8,0},{16,8},{24,16},{32,24},{40,32},{48,40},{56,48},{64,56},{72,6... | collective-permute-start | bytes 540680 | tf_op jit(solution)/shard_map/ppermute | solution.py:32
  282.0 3.0 collective-permute-done.11
  286.0 5.8 %collective-permute-start.19 = (bf16[128,704]{0,1:T(8,128)(2,1)}, bf16[128,704]{0,1:T(8,128)(2,1)}, u32[]{:S(2)}, u32[]{:S(2)}) collective-permute-start(bf16[128,704]{0,1:T(8,128)(2,1)} %collective-permute-done.18), channel_id=1, source_target_pairs={{8,0},{16,8},{24,16},{32,24},{40,32},{48,40},{56,48},{64,56},{72,6... | collective-permute-start | bytes 540680 | tf_op jit(solution)/shard_map/ppermute | solution.py:32
  291.8 3.9 collective-permute-done.12
  297.0 5.8 %collective-permute-start.20 = (bf16[128,704]{0,1:T(8,128)(2,1)}, bf16[128,704]{0,1:T(8,128)(2,1)}, u32[]{:S(2)}, u32[]{:S(2)}) collective-permute-start(bf16[128,704]{0,1:T(8,128)(2,1)} %collective-permute-done.19), channel_id=1, source_target_pairs={{8,0},{16,8},{24,16},{32,24},{40,32},{48,40},{56,48},{64,56},{72,6... | collective-permute-start | bytes 540680 | tf_op jit(solution)/shard_map/ppermute | solution.py:32
  302.8 3.2 collective-permute-done.13
  308.2 5.8 %collective-permute-start.21 = (bf16[128,704]{0,1:T(8,128)(2,1)}, bf16[128,704]{0,1:T(8,128)(2,1)S(1)}, u32[]{:S(2)}, u32[]{:S(2)}) collective-permute-start(bf16[128,704]{0,1:T(8,128)(2,1)} %collective-permute-done.20), channel_id=1, source_target_pairs={{8,0},{16,8},{24,16},{32,24},{40,32},{48,40},{56,48},{64,56},{72,6... | collective-permute-start | bytes 540680 | tf_op jit(solution)/shard_map/ppermute | solution.py:32
  314.0 3.7 collective-permute-done.14
  317.8 5.7 %collective-permute-start.22 = (bf16[128,704]{0,1:T(8,128)(2,1)S(1)}, bf16[128,704]{0,1:T(8,128)(2,1)S(1)}, u32[]{:S(2)}, u32[]{:S(2)}) collective-permute-start(bf16[128,704]{0,1:T(8,128)(2,1)S(1)} %collective-permute-done.21), channel_id=1, source_target_pairs={{8,0},{16,8},{24,16},{32,24},{40,32},{48,40},{56,48},{64,56},{72,6... | collective-permute-start | bytes 540680 | tf_op jit(solution)/shard_map/ppermute | solution.py:32
  323.5 3.2 collective-permute-done.15
  327.4 1.6 bitcast_dynamic-update-slice_fusion.14
  342.1 1.6 bitcast_dynamic-update-slice_fusion.2
  345.1 4.3 gather_fusion
  350.7 7.8 %fusion.123 = f32[1024,704]{0,1:T(8,128)} fusion(bf16[1024,2048]{1,0:T(8,128)(2,1)} %all-gather.7.cloned.1.call-done, bf16[2048,704]{0,1:T(8,128)(2,1)} %all-gather.9.cloned.1.call-done), kind=kOutput, calls=%fused_computation.222 | convolution fusion | flops 2952790016 | bytes 9961472 | tf_op jit(solution)/shard_map/dot_general | solution.py:196
  358.5 12.1 %convolution_convert_fusion.1 = bf16[1024,2048]{1,0:T(8,128)(2,1)} fusion(bf16[704,2048]{1,0:T(8,128)(2,1)} %all-gather.11.cloned.1.call-done, f32[1024,704]{0,1:T(8,128)} %fusion.123, bf16[1024,2048]{1,0:T(8,128)(2,1)} %all-gather.7.cloned.1.call-done, bf16[16,128,704]{1,2,0:T(8,128)(2,1)} %gather_fusion), kind=kOutput, calls=%fused_computation.95 | convolution fusion | flops 5912002560 | bytes 17039360 | tf_op jit(solution)/shard_map/dot_general | solution.py:200
  371.3 11.5 %reduce-scatter.10.cloned.1.call-done = bf16[512,3]{1,0:T(8,128)(2,1)} async-done(((bf16[4096,3]{1,0:T(8,128)(2,1)}), bf16[512,3]{1,0:T(8,128)(2,1)}) %reduce-scatter.10.cloned.1.call-update) | async-done | bytes 3088
  384.4 30.8 %reduce-scatter.8.cloned.1.call-done = bf16[1,128,256]{2,1,0:T(8,128)(2,1)} async-done(((bf16[8,128,256]{2,1,0:T(8,128)(2,1)}), bf16[1,128,256]{2,1,0:T(8,128)(2,1)}) %reduce-scatter.8.cloned.1.call-update) | async-done | bytes 65552 | tf_op jit(solution)/shard_map/reduce_scatter | solution.py:166
  416.7 37.7 %reduce-scatter.6.cloned.1.call-done = bf16[128,2048]{1,0:T(8,128)(2,1)} async-done(((bf16[1024,2048]{1,0:T(8,128)(2,1)}), bf16[128,2048]{1,0:T(8,128)(2,1)}) %reduce-scatter.6.cloned.1.call-update) | async-done | bytes 524304 | tf_op jit(solution)/shard_map/reduce_scatter | solution.py:199
  454.4 2.0 fusion.89
  (237 shorter events, 107.5 us)
Async XLA Ops:
  7.2 198.1 %copy-start = (f32[256]{0:T(256)S(1)}, f32[256]{0:T(256)}, u32[]{:S(2)}) copy-start(f32[256]{0:T(256)} %param.38) | copy-start | bytes 3076
  7.2 233.7 %all-gather.5.cloned.1.call-start = ((), (), s32[]{:S(2)}) async-start(), calls=%async_computation.3 | async-start | bytes 8454144 | tf_op jit(solution)/shard_map/all_gather | solution.py:182
  8.1 9.3 %collective-permute-start = (bf16[3,4096]{1,0:T(4,128)(2,1)S(1)}, bf16[3,4096]{1,0:T(4,128)(2,1)S(1)}, u32[]{:S(2)}, u32[]{:S(2)}) collective-permute-start(bf16[3,4096]{1,0:T(4,128)(2,1)S(1)} %slice_bitcast_fusion.2), channel_id=1, source_target_pairs={{0,1},{1,2},{2,3},{3,4},{4,5},{5,6},{6,7},{8,9},{9,10},{10,11},{11... | collective-permute-start | bytes 73736 | tf_op jit(solution)/shard_map/ppermute | solution.py:42
  9.4 341.2 %all-gather.9.cloned.1.call-start = ((), (), s32[]{:S(2)}) async-start(), calls=%async_computation.5 | async-start | bytes 3063808 | tf_op jit(solution)/shard_map/all_gather | solution.py:191
  24.1 83.9 %copy-start.9 = (f32[8,2,64,128]{3,0,2,1:T(8,128)}, f32[8,2,64,128]{3,0,2,1:T(8,128)S(1)}, u32[]{:S(2)}) copy-start(f32[8,2,64,128]{3,0,2,1:T(8,128)S(1)} %get-tuple-element.663) | copy-start | bytes 1572868
  24.1 85.7 %slice-start = ((f32[128,4096]{1,0:T(8,128)}), f32[128,2048]{1,0:T(8,128)S(1)}, s32[]{:S(2)}) async-start(f32[128,4096]{1,0:T(8,128)} %copy-done.2), calls=%async_computation.10 | async-start | bytes 2097152 | tf_op jit(solution)/shard_map/slice | solution.py:147
  117.0 6.5 %collective-permute-start.1 = (bf16[8,128,256]{2,1,0:T(8,128)(2,1)}, bf16[8,128,256]{2,1,0:T(8,128)(2,1)}, u32[]{:S(2)}, u32[]{:S(2)}) collective-permute-start(bf16[8,128,256]{2,1,0:T(8,128)(2,1)} %convert_element_type.129), channel_id=1, source_target_pairs={{0,1},{1,2},{2,3},{3,4},{4,5},{5,6},{6,7},{8,9},{9,10},{10,11},{11... | collective-permute-start | bytes 1572872 | tf_op jit(solution)/shard_map/ppermute | solution.py:42
  129.7 8.3 %collective-permute-start.2 = (bf16[8,128,256]{2,1,0:T(8,128)(2,1)}, bf16[8,128,256]{2,1,0:T(8,128)(2,1)}, u32[]{:S(2)}, u32[]{:S(2)}) collective-permute-start(bf16[8,128,256]{2,1,0:T(8,128)(2,1)} %convert_element_type.131), channel_id=1, source_target_pairs={{0,1},{1,2},{2,3},{3,4},{4,5},{5,6},{6,7},{8,9},{9,10},{10,11},{11... | collective-permute-start | bytes 1572872 | tf_op jit(solution)/shard_map/ppermute | solution.py:42
  144.2 10.8 %collective-permute-start.3 = (bf16[8,128,256]{2,1,0:T(8,128)(2,1)}, bf16[8,128,256]{2,1,0:T(8,128)(2,1)}, u32[]{:S(2)}, u32[]{:S(2)}) collective-permute-start(bf16[8,128,256]{2,1,0:T(8,128)(2,1)} %convert_element_type.133), channel_id=1, source_target_pairs={{0,1},{1,2},{2,3},{3,4},{4,5},{5,6},{6,7},{8,9},{9,10},{10,11},{11... | collective-permute-start | bytes 1572872 | tf_op jit(solution)/shard_map/ppermute | solution.py:42
  161.2 10.8 %collective-permute-start.4 = (bf16[8,128,256]{2,1,0:T(8,128)(2,1)}, bf16[8,128,256]{2,1,0:T(8,128)(2,1)}, u32[]{:S(2)}, u32[]{:S(2)}) collective-permute-start(bf16[8,128,256]{2,1,0:T(8,128)(2,1)} %convert_element_type.135), channel_id=1, source_target_pairs={{0,1},{1,2},{2,3},{3,4},{4,5},{5,6},{6,7},{8,9},{9,10},{10,11},{11... | collective-permute-start | bytes 1572872 | tf_op jit(solution)/shard_map/ppermute | solution.py:42
  178.2 10.8 %collective-permute-start.5 = (bf16[8,128,256]{2,1,0:T(8,128)(2,1)}, bf16[8,128,256]{2,1,0:T(8,128)(2,1)}, u32[]{:S(2)}, u32[]{:S(2)}) collective-permute-start(bf16[8,128,256]{2,1,0:T(8,128)(2,1)} %convert_element_type.137), channel_id=1, source_target_pairs={{0,1},{1,2},{2,3},{3,4},{4,5},{5,6},{6,7},{8,9},{9,10},{10,11},{11... | collective-permute-start | bytes 1572872 | tf_op jit(solution)/shard_map/ppermute | solution.py:42
  195.1 13.6 %collective-permute-start.6 = (bf16[8,128,256]{2,1,0:T(8,128)(2,1)}, bf16[8,128,256]{2,1,0:T(8,128)(2,1)}, u32[]{:S(2)}, u32[]{:S(2)}) collective-permute-start(bf16[8,128,256]{2,1,0:T(8,128)(2,1)} %convert_element_type.139), channel_id=1, source_target_pairs={{0,1},{1,2},{2,3},{3,4},{4,5},{5,6},{6,7},{8,9},{9,10},{10,11},{11... | collective-permute-start | bytes 1572872 | tf_op jit(solution)/shard_map/ppermute | solution.py:42
  204.9 145.7 %all-gather.7.cloned.1.call-start = ((), (), s32[]{:S(2)}) async-start(), calls=%async_computation.4 | async-start | bytes 4718592 | tf_op jit(solution)/shard_map/all_gather | solution.py:195
  214.1 7.6 %copy-start.4 = (f32[16,8,8,128]{3,2,1,0:T(8,128)S(1)}, f32[16,8,8,128]{3,2,1,0:T(8,128)}, u32[]{:S(2)}) copy-start(f32[16,8,8,128]{3,2,1,0:T(8,128)} %copy.263) | copy-start | bytes 1572868
  214.1 8.8 %copy-start.10 = (f32[8,2,64,128]{3,0,2,1:T(8,128)S(1)}, f32[8,2,64,128]{3,0,2,1:T(8,128)}, u32[]{:S(2)}) copy-start(f32[8,2,64,128]{3,0,2,1:T(8,128)} %copy-done.9) | copy-start | bytes 1572868
  214.2 10.6 %collective-permute-start.7 = (bf16[8,128,256]{2,1,0:T(8,128)(2,1)S(1)}, bf16[8,128,256]{2,1,0:T(8,128)(2,1)S(1)}, u32[]{:S(2)}, u32[]{:S(2)}) collective-permute-start(bf16[8,128,256]{2,1,0:T(8,128)(2,1)S(1)} %convert_element_type.141), channel_id=1, source_target_pairs={{0,1},{1,2},{2,3},{3,4},{4,5},{5,6},{6,7},{8,9},{9,10},{10,11},{11... | collective-permute-start | bytes 1572872 | tf_op jit(solution)/shard_map/ppermute | solution.py:42
  224.9 2.3 copy-start.6
  230.3 2.3 copy-start.3
  230.3 2.3 copy-start.6
  235.7 3.2 copy-start.8
  240.9 5.9 %copy-start.18 = (f32[2048]{0:T(1024)S(1)}, f32[2048]{0:T(1024)}, u32[]{:S(2)}) copy-start(f32[2048]{0:T(1024)} %param.40) | copy-start | bytes 24580
  240.9 7.5 %copy-start.11 = (bf16[128,704]{0,1:T(8,128)(2,1)S(1)}, bf16[128,704]{0,1:T(8,128)(2,1)}, u32[]{:S(2)}) copy-start(bf16[128,704]{0,1:T(8,128)(2,1)} %param.42) | copy-start | bytes 540676
  240.9 65.1 %copy-start.5 = (bf16[1,128,4096]{2,1,0:T(8,128)(2,1)S(1)}, bf16[1,128,4096]{2,1,0:T(8,128)(2,1)}, u32[]{:S(2)}) copy-start(bf16[1,128,4096]{2,1,0:T(8,128)(2,1)} %param.30) | copy-start | bytes 3145732
  247.7 110.8 %all-gather.11.cloned.1.call-start = ((), (), s32[]{:S(2)}) async-start(), calls=%async_computation.6 | async-start | bytes 3063808 | tf_op jit(solution)/shard_map/all_gather | solution.py:194
  248.3 134.5 %reduce-scatter.10.cloned.1.call-start = ((), (), s32[]{:S(2)}) async-start(), calls=%async_computation.9 | async-start | bytes 1179648
  248.4 9.7 %collective-permute-start.8 = (bf16[128,704]{0,1:T(8,128)(2,1)S(1)}, bf16[128,704]{0,1:T(8,128)(2,1)S(1)}, u32[]{:S(2)}, u32[]{:S(2)}) collective-permute-start(bf16[128,704]{0,1:T(8,128)(2,1)S(1)} %copy-done.11), channel_id=1, source_target_pairs={{0,8},{8,16},{16,24},{24,32},{32,40},{40,48},{48,56},{56,64},{64,7... | collective-permute-start | bytes 540680 | tf_op jit(solution)/shard_map/ppermute | solution.py:30
  258.1 8.8 %collective-permute-start.9 = (bf16[128,704]{0,1:T(8,128)(2,1)S(1)}, bf16[128,704]{0,1:T(8,128)(2,1)S(1)}, u32[]{:S(2)}, u32[]{:S(2)}) collective-permute-start(bf16[128,704]{0,1:T(8,128)(2,1)S(1)} %collective-permute-done.8), channel_id=1, source_target_pairs={{0,8},{8,16},{16,24},{24,32},{32,40},{40,48},{48,56},{56,64},{64,7... | collective-permute-start | bytes 540680 | tf_op jit(solution)/shard_map/ppermute | solution.py:30
  258.1 8.8 %collective-permute-start.16 = (bf16[128,704]{0,1:T(8,128)(2,1)S(1)}, bf16[128,704]{0,1:T(8,128)(2,1)S(1)}, u32[]{:S(2)}, u32[]{:S(2)}) collective-permute-start(bf16[128,704]{0,1:T(8,128)(2,1)S(1)} %copy-done.11), channel_id=1, source_target_pairs={{8,0},{16,8},{24,16},{32,24},{40,32},{48,40},{56,48},{64,56},{72,6... | collective-permute-start | bytes 540680 | tf_op jit(solution)/shard_map/ppermute | solution.py:32
  266.9 9.2 %copy-start.14 = (bf16[128,704]{0,1:T(8,128)(2,1)}, bf16[128,704]{0,1:T(8,128)(2,1)S(1)}, u32[]{:S(2)}) copy-start(bf16[128,704]{0,1:T(8,128)(2,1)S(1)} %collective-permute-done.9) | copy-start | bytes 540676
  266.9 8.8 %collective-permute-start.10 = (bf16[128,704]{0,1:T(8,128)(2,1)S(1)}, bf16[128,704]{0,1:T(8,128)(2,1)S(1)}, u32[]{:S(2)}, u32[]{:S(2)}) collective-permute-start(bf16[128,704]{0,1:T(8,128)(2,1)S(1)} %collective-permute-done.9), channel_id=1, source_target_pairs={{0,8},{8,16},{16,24},{24,32},{32,40},{40,48},{48,56},{56,64},{64,7... | collective-permute-start | bytes 540680 | tf_op jit(solution)/shard_map/ppermute | solution.py:30
  267.6 8.5 %collective-permute-start.17 = (bf16[128,704]{0,1:T(8,128)(2,1)S(1)}, bf16[128,704]{0,1:T(8,128)(2,1)}, u32[]{:S(2)}, u32[]{:S(2)}) collective-permute-start(bf16[128,704]{0,1:T(8,128)(2,1)S(1)} %collective-permute-done.16), channel_id=1, source_target_pairs={{8,0},{16,8},{24,16},{32,24},{40,32},{48,40},{56,48},{64,56},{72,6... | collective-permute-start | bytes 540680 | tf_op jit(solution)/shard_map/ppermute | solution.py:32
  275.7 6.3 %copy-start.16 = (bf16[128,704]{0,1:T(8,128)(2,1)}, bf16[128,704]{0,1:T(8,128)(2,1)S(1)}, u32[]{:S(2)}) copy-start(bf16[128,704]{0,1:T(8,128)(2,1)S(1)} %collective-permute-done.10) | copy-start | bytes 540676
  275.7 9.3 %collective-permute-start.11 = (bf16[128,704]{0,1:T(8,128)(2,1)S(1)}, bf16[128,704]{0,1:T(8,128)(2,1)}, u32[]{:S(2)}, u32[]{:S(2)}) collective-permute-start(bf16[128,704]{0,1:T(8,128)(2,1)S(1)} %collective-permute-done.10), channel_id=1, source_target_pairs={{0,8},{8,16},{16,24},{24,32},{32,40},{40,48},{48,56},{56,64},{64,7... | collective-permute-start | bytes 540680 | tf_op jit(solution)/shard_map/ppermute | solution.py:30
  276.1 9.9 %collective-permute-start.18 = (bf16[128,704]{0,1:T(8,128)(2,1)}, bf16[128,704]{0,1:T(8,128)(2,1)}, u32[]{:S(2)}, u32[]{:S(2)}) collective-permute-start(bf16[128,704]{0,1:T(8,128)(2,1)} %collective-permute-done.17), channel_id=1, source_target_pairs={{8,0},{16,8},{24,16},{32,24},{40,32},{48,40},{56,48},{64,56},{72,6... | collective-permute-start | bytes 540680 | tf_op jit(solution)/shard_map/ppermute | solution.py:32
  285.0 10.7 %collective-permute-start.12 = (bf16[128,704]{0,1:T(8,128)(2,1)}, bf16[128,704]{0,1:T(8,128)(2,1)}, u32[]{:S(2)}, u32[]{:S(2)}) collective-permute-start(bf16[128,704]{0,1:T(8,128)(2,1)} %collective-permute-done.11), channel_id=1, source_target_pairs={{0,8},{8,16},{16,24},{24,32},{32,40},{40,48},{48,56},{56,64},{64,7... | collective-permute-start | bytes 540680 | tf_op jit(solution)/shard_map/ppermute | solution.py:30
  286.0 11.0 %collective-permute-start.19 = (bf16[128,704]{0,1:T(8,128)(2,1)}, bf16[128,704]{0,1:T(8,128)(2,1)}, u32[]{:S(2)}, u32[]{:S(2)}) collective-permute-start(bf16[128,704]{0,1:T(8,128)(2,1)} %collective-permute-done.18), channel_id=1, source_target_pairs={{8,0},{16,8},{24,16},{32,24},{40,32},{48,40},{56,48},{64,56},{72,6... | collective-permute-start | bytes 540680 | tf_op jit(solution)/shard_map/ppermute | solution.py:32
  295.7 10.3 %collective-permute-start.13 = (bf16[128,704]{0,1:T(8,128)(2,1)}, bf16[128,704]{0,1:T(8,128)(2,1)}, u32[]{:S(2)}, u32[]{:S(2)}) collective-permute-start(bf16[128,704]{0,1:T(8,128)(2,1)} %collective-permute-done.12), channel_id=1, source_target_pairs={{0,8},{8,16},{16,24},{24,32},{32,40},{40,48},{48,56},{56,64},{64,7... | collective-permute-start | bytes 540680 | tf_op jit(solution)/shard_map/ppermute | solution.py:30
  297.0 11.2 %collective-permute-start.20 = (bf16[128,704]{0,1:T(8,128)(2,1)}, bf16[128,704]{0,1:T(8,128)(2,1)}, u32[]{:S(2)}, u32[]{:S(2)}) collective-permute-start(bf16[128,704]{0,1:T(8,128)(2,1)} %collective-permute-done.19), channel_id=1, source_target_pairs={{8,0},{16,8},{24,16},{32,24},{40,32},{48,40},{56,48},{64,56},{72,6... | collective-permute-start | bytes 540680 | tf_op jit(solution)/shard_map/ppermute | solution.py:32
  306.0 11.7 %collective-permute-start.14 = (bf16[128,704]{0,1:T(8,128)(2,1)}, bf16[128,704]{0,1:T(8,128)(2,1)}, u32[]{:S(2)}, u32[]{:S(2)}) collective-permute-start(bf16[128,704]{0,1:T(8,128)(2,1)} %collective-permute-done.13), channel_id=1, source_target_pairs={{0,8},{8,16},{16,24},{24,32},{32,40},{40,48},{48,56},{56,64},{64,7... | collective-permute-start | bytes 540680 | tf_op jit(solution)/shard_map/ppermute | solution.py:30
  306.3 27.6 %copy-start.17 = (bf16[128,704]{0,1:T(8,128)(2,1)S(1)}, bf16[128,704]{0,1:T(8,128)(2,1)}, u32[]{:S(2)}) copy-start(bf16[128,704]{0,1:T(8,128)(2,1)} %copy-done.16) | copy-start | bytes 540676
  306.3 28.3 %copy-start.15 = (bf16[128,704]{0,1:T(8,128)(2,1)S(1)}, bf16[128,704]{0,1:T(8,128)(2,1)}, u32[]{:S(2)}) copy-start(bf16[128,704]{0,1:T(8,128)(2,1)} %copy-done.14) | copy-start | bytes 540676
  306.3 30.3 %copy-start.13 = (bf16[128,704]{0,1:T(8,128)(2,1)S(1)}, bf16[128,704]{0,1:T(8,128)(2,1)}, u32[]{:S(2)}) copy-start(bf16[128,704]{0,1:T(8,128)(2,1)} %copy-done.12) | copy-start | bytes 540676
  307.7 107.5 %reduce-scatter.8.cloned.1.call-start = ((), (), s32[]{:S(2)}) async-start(), calls=%async_computation.8 | async-start | bytes 589824 | tf_op jit(solution)/shard_map/reduce_scatter | solution.py:166
  308.2 9.6 %collective-permute-start.21 = (bf16[128,704]{0,1:T(8,128)(2,1)}, bf16[128,704]{0,1:T(8,128)(2,1)S(1)}, u32[]{:S(2)}, u32[]{:S(2)}) collective-permute-start(bf16[128,704]{0,1:T(8,128)(2,1)} %collective-permute-done.20), channel_id=1, source_target_pairs={{8,0},{16,8},{24,16},{32,24},{40,32},{48,40},{56,48},{64,56},{72,6... | collective-permute-start | bytes 540680 | tf_op jit(solution)/shard_map/ppermute | solution.py:32
  317.7 9.0 %collective-permute-start.15 = (bf16[128,704]{0,1:T(8,128)(2,1)}, bf16[128,704]{0,1:T(8,128)(2,1)S(1)}, u32[]{:S(2)}, u32[]{:S(2)}) collective-permute-start(bf16[128,704]{0,1:T(8,128)(2,1)} %collective-permute-done.14), channel_id=1, source_target_pairs={{0,8},{8,16},{16,24},{24,32},{32,40},{40,48},{48,56},{56,64},{64,7... | collective-permute-start | bytes 540680 | tf_op jit(solution)/shard_map/ppermute | solution.py:30
  317.8 26.7 %collective-permute-start.22 = (bf16[128,704]{0,1:T(8,128)(2,1)S(1)}, bf16[128,704]{0,1:T(8,128)(2,1)S(1)}, u32[]{:S(2)}, u32[]{:S(2)}) collective-permute-start(bf16[128,704]{0,1:T(8,128)(2,1)S(1)} %collective-permute-done.21), channel_id=1, source_target_pairs={{8,0},{16,8},{24,16},{32,24},{40,32},{48,40},{56,48},{64,56},{72,6... | collective-permute-start | bytes 540680 | tf_op jit(solution)/shard_map/ppermute | solution.py:32
  350.3 104.1 %reduce-scatter.6.cloned.1.call-start = ((), (), s32[]{:S(2)}) async-start(), calls=%async_computation.7 | async-start | bytes 4718592 | tf_op jit(solution)/shard_map/reduce_scatter | solution.py:199
  370.6 85.8 %copy-start.1 = (f32[256]{0:T(256)S(1)}, f32[256]{0:T(256)}, u32[]{:S(2)}) copy-start(f32[256]{0:T(256)} %param.38) | copy-start | bytes 3076
  (5 other events, 6.7 us)
Sparse Core Ops, SparseCore 0:
  11.0 74.2 all-gather.4
  205.1 56.5 all-gather.8
  264.0 29.6 all-gather.6
  295.7 51.7 all-gather.10
  349.7 33.0 reduce-scatter.9
  385.0 30.1 reduce-scatter.7
  417.6 36.7 reduce-scatter.5
